TPU v7x, 256 devices: a whole 4x4x8 slice. The times are simulated.
256 devices in a mesh: dp: 32 (over z, x), tensor: 8 (over y, core).
Axes of the slice: x: 4, y: 4, z: 8, core: 2. Of those that a mesh axis runs over, the one named last changes fastest.
Arguments:
- tokens: bfloat16 [65536, 8192], P('dp', 'tensor'), may hold values from -6 to 6
- base_value_weight: bfloat16 [8192, 1024], P('tensor'), may hold values from -0.0625 to 0.0625
- adapter_down_weight: bfloat16 [512, 8192, 64], P('dp', 'tensor'), may hold values from -0.0625 to 0.0625
- adapter_up_weight: bfloat16 [512, 64, 1024], P('dp', None, 'tensor'), may hold values from -0.75 to 0.75
- request_adapter_index: int32 [128], P('dp'), may hold values from 0 to 511
- storage_index_table: int32 [512], replicated, may hold values from 0 to 511, each once
Outputs:
- values_out: bfloat16 [65536, 1024], P('dp', 'tensor')
Inputs may be any that keep to these rules, and one draw needn't show every extreme that they name: `request_adapter_index`: each adapter id names an adapter. storage_index_table is a permutation of the storage positions.
All inputs are finite; a program needn't handle non-finite values.
Results may differ from a plain program's by a relative error of at most 0.003.
Values may be sent and summed in bfloat16 or wider, within the bound.
A program may use at most 128 MiB of HBM per device.

v0:
```python
import jax
import jax.numpy as jnp
from jax import lax
from jax.sharding import PartitionSpec as P

adapter_scale = 0.5


def shards(
    tokens,
    base_value_weight,
    adapter_down_weight,
    adapter_up_weight,
    request_adapter_index,
    storage_index_table,
):
    n_rows, width = tokens.shape
    requests_here = request_adapter_index.shape[0]
    seq_len = n_rows // requests_here
    owned = adapter_down_weight.shape[0]
    rank = adapter_down_weight.shape[2]
    local_columns = adapter_up_weight.shape[2]
    n_dp = lax.axis_size("dp")
    down_t = jnp.swapaxes(adapter_down_weight, 1, 2)
    pieces = jnp.concatenate(
        (
            down_t.reshape(owned, n_dp, rank * width // n_dp // 128, 128),
            adapter_up_weight.reshape(owned, n_dp, rank * local_columns // n_dp // 128, 128),
        ),
        axis=2,
    )
    pieces = jnp.swapaxes(pieces, 0, 1)
    held = lax.all_to_all(pieces, "dp", split_axis=0, concat_axis=0, tiled=True)
    held = held.reshape(n_dp * owned, -1, 128)
    every_id = lax.all_gather(request_adapter_index, "dp", axis=0, tiled=True)
    positions = storage_index_table[every_id]
    outgoing = held[positions].reshape(n_dp, requests_here, -1, 128)
    fetched = lax.all_to_all(outgoing, "dp", split_axis=0, concat_axis=0, tiled=True)
    fetched = jnp.swapaxes(fetched, 0, 1)
    down_rows = rank * width // n_dp // 128
    down_sel = fetched[:, :, :down_rows].reshape(requests_here, rank, width)
    up_sel = fetched[:, :, down_rows:].reshape(requests_here, rank, local_columns)
    base_projection = lax.psum_scatter(
        lax.dot_general(
            base_value_weight, tokens, (((0,), (1,)), ((), ())), preferred_element_type=jnp.float32
        ),
        "tensor",
        scatter_dimension=0,
        tiled=True,
    ).T
    grouped = tokens.reshape(requests_here, seq_len, width)
    low_part = jnp.einsum("rsd,rkd->rks", grouped, down_sel, preferred_element_type=jnp.float32)
    low = lax.psum(low_part, "tensor").astype(jnp.bfloat16)
    adapter_update = jnp.einsum("rks,rkc->rsc", low, up_sel, preferred_element_type=jnp.float32)
    adapter_update = adapter_update.reshape(n_rows, local_columns)
    return (base_projection + adapter_scale * adapter_update).astype(jnp.bfloat16)


def solution(mesh):
    return jax.shard_map(
        shards,
        mesh=mesh,
        in_specs=(
            P("dp", "tensor"),
            P("tensor", None),
            P("dp", "tensor", None),
            P("dp", None, "tensor"),
            P("dp"),
            P(),
        ),
        out_specs=P("dp", "tensor"),
        check_vma=False,
    )
```

profile of v0, /device:TPU:2, one launch (start us, length us, event | category | flops | bytes accessed | tf_op | source)
XLA Modules:
  0.0 181.0 jit_solution(14180586535549913768)
XLA Ops:
  6.5 0.0 copy-start
  6.5 0.0 reduce-scatter.2.cloned.1.call-start
  6.5 1.6 copy-done
  8.1 9.0 %fusion.3 = f32[1024,2048]{1,0:T(8,128)} fusion(bf16[1024,1024]{1,0:T(8,128)(2,1)S(1)} %copy-done, bf16[2048,1024]{1,0:T(8,128)(2,1)} %param.6), kind=kOutput, calls=%fused_computation.12 | convolution fusion | flops 4294967296 | bytes 14680064 | tf_op jit(solution)/shard_map/dot_general | solution.py:44
  17.1 0.0 reduce-scatter.2.cloned.1.call-update
  17.1 0.0 copy-start.2
  17.1 4.2 %reshape.37 = bf16[16,32,16,128]{3,2,1,0:T(8,128)(2,1)} reshape(bf16[16,64,1024]{2,1,0:T(8,128)(2,1)} %bitcast.33) | data formatting | bytes 4194304 | tf_op jit(solution)/shard_map/reshape | solution.py:27
  21.4 2.4 %maximum_bitcast_fusion = bf16[32,16,18,128]{3,2,0,1:T(8,128)(2,1)S(1)} fusion(bf16[16,32,2,128]{3,2,1,0:T(2,128)(2,1)S(1)} %bitcast.35, bf16[16,32,16,128]{3,2,1,0:T(8,128)(2,1)} %reshape.37), kind=kLoop, calls=%fused_computation.2 | loop fusion | flops 4718592 | bytes 4718592 | tf_op jit(solution)/shard_map/transpose | solution.py:32
  23.8 4.2 %copy.23 = bf16[32,16,18,128]{3,1,2,0:T(8,128)(2,1)} copy(bf16[32,16,18,128]{3,2,0,1:T(8,128)(2,1)S(1)} %maximum_bitcast_fusion) | data formatting | bytes 4718592 | tf_op jit(solution)/shard_map/transpose | solution.py:32
  28.0 11.8 %all-to-all-start = ((bf16[32,16,18,128]{3,1,2,0:T(8,128)(2,1)}), bf16[32,16,18,128]{3,1,2,0:T(8,128)(2,1)}, u32[]{:S(2)}, u32[]{:S(2)}) async-start(bf16[32,16,18,128]{3,1,2,0:T(8,128)(2,1)} %copy.23), calls=%async_computation.1 | async-start | bytes 4718592 | tf_op jit(solution)/shard_map/all_to_all | solution.py:33
  39.8 0.0 copy-done.4
  39.8 0.6 dynamic-slice
  41.0 0.2 dynamic-update-slice
  41.3 57.8 %all-reduce = s32[128]{0:T(128)S(1)} all-reduce(s32[128]{0:T(128)S(1)} %dynamic-update-slice), channel_id=1, replica_groups=mesh['dp'=32,'tensor'=8] {'dp'}, use_global_device_ids=true, to_apply=%add | all-reduce | flops 128 | bytes 1024
  99.1 1.3 gather_fusion
  100.4 0.0 all-to-all-done
  100.4 2.3 %copy.24 = bf16[32,16,18,128]{3,1,0,2:T(8,128)(2,1)S(1)} copy(bf16[32,16,18,128]{3,1,2,0:T(8,128)(2,1)} %all-to-all-done) | data formatting | bytes 4718592 | tf_op jit(solution)/shard_map/all_to_all | solution.py:33
  102.7 3.4 %copy.25 = bf16[512,18,128]{2,1,0:T(8,128)(2,1)} copy(bf16[512,18,128]{2,0,1:T(8,128)(2,1)S(1)} %bitcast.27) | data formatting | bytes 4718592 | tf_op jit(solution)/shard_map/reshape | solution.py:34
  106.1 2.6 %gather_fusion.1 = bf16[128,18,128]{2,1,0:T(8,128)(2,1)S(1)} fusion(bf16[512,18,128]{2,1,0:T(8,128)(2,1)} %copy.25, s32[1024]{0:T(1024)S(1)} %pad_clamp_fusion), kind=kCustom, calls=%fused_computation.1 | custom fusion | bytes 1180160 | tf_op jit(solution)/shard_map/gather | solution.py:37
  108.7 0.2 copy.27
  108.9 24.5 %all_to_all.10 = bf16[32,4,18,128]{3,1,2,0:T(4,128)(2,1)S(1)} all-to-all(bf16[32,4,18,128]{3,1,2,0:T(4,128)(2,1)S(1)} %copy.27), channel_id=1, replica_groups=mesh['dp'=32,'tensor'=8] {'dp'}, dimensions={0} | all-to-all | bytes 1179648 | tf_op jit(solution)/shard_map/all_to_all | solution.py:38
  133.5 0.3 slice.12
  133.8 0.1 copy.28
  133.8 0.2 reshape.41
  134.1 3.6 %fusion.4 = f32[4,64,512]{2,1,0:T(8,128)S(1)} fusion(bf16[4,64,1024]{2,1,0:T(8,128)(2,1)S(1)} %reshape.41, bf16[4,512,1024]{2,1,0:T(8,128)(2,1)} %bitcast.28), kind=kOutput, calls=%fused_computation.13 | convolution fusion | flops 268435456 | bytes 5242880 | tf_op jit(solution)/shard_map/rsd,rkd->rks/dot_general | solution.py:52
  137.6 0.1 copy.29
  137.7 29.3 %all-reduce.2 = bf16[4,64,512]{2,1,0:T(8,128)(2,1)S(1)} all-reduce(f32[4,64,512]{2,1,0:T(8,128)S(1)} %fusion.4), channel_id=1, replica_groups=mesh['dp'=32,'tensor'=8] {'tensor'}, use_global_device_ids=true, to_apply=%region_1.0 | all-reduce | flops 131072 | bytes 786432 | tf_op jit(solution)/shard_map/psum | solution.py:53
  167.0 1.4 convolution_multiply_fusion
  168.4 1.6 copy.35
  170.0 0.0 reduce-scatter.2.cloned.1.call-done
  170.0 2.1 %fusion = bf16[2048,128]{0,1:T(8,128)(2,1)} fusion(f32[2048,128]{0,1:T(8,128)S(1)} %copy.35, f32[128,2048]{1,0:T(8,128)} %reduce-scatter.2.cloned.1.call-done), kind=kLoop, calls=%fused_computation.5 | loop fusion | flops 524288 | bytes 2621440 | tf_op jit(solution)/shard_map/convert_element_type | solution.py:56
  172.1 2.0 %copy.31 = bf16[2048,128]{1,0:T(8,128)(2,1)} copy(bf16[2048,128]{0,1:T(8,128)(2,1)} %fusion) | data formatting | bytes 1048576 | tf_op jit(solution)/shard_map/convert_element_type | solution.py:56
  (12 shorter events, 0.1 us)
Async XLA Ops:
  6.5 1.6 copy-start
  6.5 163.4 %reduce-scatter.2.cloned.1.call-start = ((), (), s32[]{:S(2)}) async-start(), calls=%async_computation.3 | async-start | bytes 9437184 | tf_op jit(solution)/shard_map/reduce_scatter | solution.py:43
  17.1 4.3 %copy-start.2 = (bf16[16,64,128]{2,1,0:T(8,128)(2,1)S(1)}, bf16[16,64,128]{2,1,0:T(8,128)(2,1)}, u32[]{:S(2)}) copy-start(bf16[16,64,128]{2,1,0:T(8,128)(2,1)} %param.9) | copy-start | bytes 786436
  27.9 11.8 %copy-start.4 = (u32[256]{0:T(256)S(1)}, u32[256]{0:T(256)}, u32[]{:S(2)}) copy-start(u32[256]{0:T(256)} %constant.11) | copy-start | bytes 3076
  28.0 13.1 %copy-start.3 = (s32[4]{0:T(128)S(1)}, s32[4]{0:T(128)}, u32[]{:S(2)}) copy-start(s32[4]{0:T(128)} %param.10) | copy-start | bytes 52
  28.0 71.1 %copy-start.1 = (s32[512]{0:T(512)S(1)}, s32[512]{0:T(512)}, u32[]{:S(2)}) copy-start(s32[512]{0:T(512)} %param.11) | copy-start | bytes 6148
  28.0 72.4 %all-to-all-start = ((bf16[32,16,18,128]{3,1,2,0:T(8,128)(2,1)}), bf16[32,16,18,128]{3,1,2,0:T(8,128)(2,1)}, u32[]{:S(2)}, u32[]{:S(2)}) async-start(bf16[32,16,18,128]{3,1,2,0:T(8,128)(2,1)} %copy.23), calls=%async_computation.1 | async-start | bytes 4718592 | tf_op jit(solution)/shard_map/all_to_all | solution.py:33
Sparse Core Ops, SparseCore 0:
  17.2 57.9 reduce-scatter.1
where the time goes:
time: 182 us; the launch traced here: 181 us
  blocking collectives  112 us (62%)
  local copies, waits for them, and re-layouts  24.9 us (14%)
  between operations  14.2 us (8%)
  matrix products  13.9 us (8%)
  starting transfers between devices  11.8 us (6%)
  other arithmetic  4.53 us (2%)
    unnamed x1, blocking collectives  57.8 us
    psum x1, blocking collectives, shards(): low = lax.psum(low_part, 'tensor').astype(jnp.bfloat16)  29.3 us
    all_to_all x1, blocking collectives, shards(): lax.all_to_all(outgoing, 'dp', split_axis=0, concat_axis=0, tiled=True)  24.5 us
    all_to_all x1, starting transfers between devices, shards(): held = lax.all_to_all(pieces, 'dp', split_axis=0, concat_axis=0, tiled=True)  11.8 us
    dot_general x1, matrix products, shards(): lax.dot_general(base_value_weight, tokens, (((0,), (1,)), ((), ())), pref...  8.96 us
    reshape x1, local copies, waits for them, and re-layouts, shards(): down_t.reshape(owned, n_dp, rank * width // n_dp // 128, 128)  4.24 us
    transpose x1, local copies, waits for them, and re-layouts, shards(): pieces = jnp.swapaxes(pieces, 0, 1)  4.18 us
  transfers between devices with their start and end apart: 2, of which 0 were waited for; matrix products, arithmetic and copies ran while one was open for 16% of the time, Pallas kernels for 0%

commit v1 on v0

--- a/solution.py
+++ b/solution.py
@@ -50,7 +50,7 @@
     ).T
     grouped = tokens.reshape(requests_here, seq_len, width)
     low_part = jnp.einsum("rsd,rkd->rks", grouped, down_sel, preferred_element_type=jnp.float32)
-    low = lax.psum(low_part, "tensor").astype(jnp.bfloat16)
+    low = jnp.sum(lax.all_gather(low_part, "tensor"), axis=0).astype(jnp.bfloat16)
     adapter_update = jnp.einsum("rks,rkc->rsc", low, up_sel, preferred_element_type=jnp.float32)
     adapter_update = adapter_update.reshape(n_rows, local_columns)
     return (base_projection + adapter_scale * adapter_update).astype(jnp.bfloat16)

time: 182 us -> 231 us (1.27)
  waiting for transfers between devices: 0.04 us -> 74.3 us
  blocking collectives: 112 us -> 82.2 us
  other arithmetic: 4.53 us -> 7.24 us
    reduce_scatter x1, waiting for transfers between devices: 0.02 us -> 51.9 us  [shards(): lax.psum_scatter(lax.dot_general(base_value_weight, tokens, (((0,), (1,))...]
    psum x1 -> x0, blocking collectives: 29.3 us -> none  [shards(): low = lax.psum(low_part, 'tensor').astype(jnp.bfloat16)]
    all_gather x0 -> x1, waiting for transfers between devices: none -> 22.4 us  [shards(): lax.all_gather(low_part, 'tensor')]
    reduce_sum x0 -> x1, other arithmetic: none -> 2.69 us  [shards(): jnp.sum(lax.all_gather(low_part, 'tensor'), axis=0).astype(jnp.bfloat16)]
  transfers between devices with their start and end apart: 2 -> 3, of which waited for: 0 -> 2; matrix products, arithmetic and copies ran while one was open for 16% -> 7% of each run, Pallas kernels for 0% -> 0%
where the time goes in v1:
time: 231 us; the launch traced here: 230 us
  blocking collectives  82.2 us (36%)
  waiting for transfers between devices  74.3 us (32%)
  local copies, waits for them, and re-layouts  25 us (11%)
  matrix products  14.8 us (6%)
  between operations  14.2 us (6%)
  starting transfers between devices  12.1 us (5%)
  other arithmetic  7.24 us (3%)
    unnamed x1, blocking collectives  57.7 us
    reduce_scatter x1, waiting for transfers between devices, shards(): lax.psum_scatter(lax.dot_general(base_value_weight, tokens, (((0,), (1,))...  51.9 us
    all_to_all x1, blocking collectives, shards(): lax.all_to_all(outgoing, 'dp', split_axis=0, concat_axis=0, tiled=True)  24.5 us
    all_gather x1, waiting for transfers between devices, shards(): lax.all_gather(low_part, 'tensor')  22.4 us
    all_to_all x1, starting transfers between devices, shards(): held = lax.all_to_all(pieces, 'dp', split_axis=0, concat_axis=0, tiled=True)  11.8 us
    dot_general x1, matrix products, shards(): lax.dot_general(base_value_weight, tokens, (((0,), (1,)), ((), ())), pref...  8.99 us
  transfers between devices with their start and end apart: 3, of which 2 were waited for; matrix products, arithmetic and copies ran while one was open for 7% of the time, Pallas kernels for 0%

profile of v1, /device:TPU:2, one launch (start us, length us, event | category | flops | bytes accessed | tf_op | source)
XLA Modules:
  0.0 229.9 jit_solution(12391628966867068021)
XLA Ops:
  6.5 4.3 %reshape.37 = bf16[16,32,16,128]{3,2,1,0:T(8,128)(2,1)} reshape(bf16[16,64,1024]{2,1,0:T(8,128)(2,1)} %bitcast.35) | data formatting | bytes 4194304 | tf_op jit(solution)/shard_map/reshape | solution.py:27
  10.8 2.4 %maximum_bitcast_fusion = bf16[32,16,18,128]{3,2,0,1:T(8,128)(2,1)S(1)} fusion(bf16[16,32,2,128]{3,2,1,0:T(2,128)(2,1)S(1)} %bitcast.37, bf16[16,32,16,128]{3,2,1,0:T(8,128)(2,1)} %reshape.37), kind=kLoop, calls=%fused_computation.2 | loop fusion | flops 4718592 | bytes 4718592 | tf_op jit(solution)/shard_map/transpose | solution.py:32
  13.2 4.1 %copy.24 = bf16[32,16,18,128]{3,1,2,0:T(8,128)(2,1)} copy(bf16[32,16,18,128]{3,2,0,1:T(8,128)(2,1)S(1)} %maximum_bitcast_fusion) | data formatting | bytes 4718592 | tf_op jit(solution)/shard_map/transpose | solution.py:32
  17.4 11.8 %all-to-all-start = ((bf16[32,16,18,128]{3,1,2,0:T(8,128)(2,1)}), bf16[32,16,18,128]{3,1,2,0:T(8,128)(2,1)}, u32[]{:S(2)}, u32[]{:S(2)}) async-start(bf16[32,16,18,128]{3,1,2,0:T(8,128)(2,1)} %copy.24), calls=%async_computation.1 | async-start | bytes 4718592 | tf_op jit(solution)/shard_map/all_to_all | solution.py:33
  29.2 0.0 all-gather.3.cloned.1.call-start
  29.3 0.6 dynamic-slice
  30.5 0.2 dynamic-update-slice
  30.8 57.7 %all-reduce = s32[128]{0:T(128)S(1)} all-reduce(s32[128]{0:T(128)S(1)} %dynamic-update-slice), channel_id=1, replica_groups=mesh['dp'=32,'tensor'=8] {'dp'}, use_global_device_ids=true, to_apply=%add | all-reduce | flops 128 | bytes 1024
  88.5 0.0 copy-done.1
  88.5 1.3 gather_fusion
  89.8 0.0 all-to-all-done
  89.8 2.3 copy.25
  92.1 3.3 %copy.26 = bf16[512,18,128]{2,1,0:T(8,128)(2,1)} copy(bf16[512,18,128]{2,0,1:T(8,128)(2,1)S(1)} %bitcast.28) | data formatting | bytes 4718592 | tf_op jit(solution)/shard_map/reshape | solution.py:34
  95.4 2.6 %gather_fusion.1 = bf16[128,18,128]{2,1,0:T(8,128)(2,1)S(1)} fusion(bf16[512,18,128]{2,1,0:T(8,128)(2,1)} %copy.26, s32[1024]{0:T(1024)S(1)} %pad_clamp_fusion), kind=kCustom, calls=%fused_computation.1 | custom fusion | bytes 1180160 | tf_op jit(solution)/shard_map/gather | solution.py:37
  98.0 0.2 copy.28
  98.3 24.5 %all_to_all.10 = bf16[32,4,18,128]{3,1,2,0:T(4,128)(2,1)S(1)} all-to-all(bf16[32,4,18,128]{3,1,2,0:T(4,128)(2,1)S(1)} %copy.28), channel_id=1, replica_groups=mesh['dp'=32,'tensor'=8] {'dp'}, dimensions={0} | all-to-all | bytes 1179648 | tf_op jit(solution)/shard_map/all_to_all | solution.py:38
  122.8 0.3 slice.12
  123.0 0.9 copy.29
  123.9 1.3 reshape.41
  125.2 4.4 %fusion.4 = f32[4,64,512]{2,1,0:T(8,128)} fusion(bf16[4,64,1024]{2,1,0:T(8,128)(2,1)S(1)} %reshape.41, bf16[4,512,1024]{2,1,0:T(8,128)(2,1)} %bitcast.29), kind=kOutput, calls=%fused_computation.13 | convolution fusion | flops 268435456 | bytes 5242880 | tf_op jit(solution)/shard_map/rsd,rkd->rks/dot_general | solution.py:52
  129.6 0.0 all-gather.3.cloned.1.call-update
  129.6 0.2 reduce-scatter.2.cloned.1.call-start
  129.8 9.0 %fusion.3 = f32[1024,2048]{1,0:T(8,128)} fusion(bf16[1024,1024]{1,0:T(8,128)(2,1)S(1)} %copy-done, bf16[2048,1024]{1,0:T(8,128)(2,1)} %param.6), kind=kOutput, calls=%fused_computation.12 | convolution fusion | flops 4294967296 | bytes 14680064 | tf_op jit(solution)/shard_map/dot_general | solution.py:44
  138.8 0.0 reduce-scatter.2.cloned.1.call-update
  138.9 0.1 copy.30
  138.9 22.4 %all-gather.3.cloned.1.call-done = f32[32,64,512]{2,1,0:T(8,128)} async-done(((f32[4,64,512]{2,1,0:T(8,128)}), f32[32,64,512]{2,1,0:T(8,128)}) %all-gather.3.cloned.1.call-update) | async-done | bytes 4194320 | tf_op jit(solution)/shard_map/all_gather | solution.py:53
  161.3 2.7 %reduce_sum.9 = bf16[4,64,512]{2,1,0:T(8,128)(2,1)S(1)} reduce(f32[8,4,64,512]{3,2,1,0:T(8,128)} %bitcast.30, f32[]{:T(128)} %constant.2.clone.1), dimensions={0}, to_apply=%region_1.0 | reduce | flops 917504 | bytes 4456452 | tf_op jit(solution)/shard_map/reduce_sum | solution.py:53
  164.0 1.4 convolution_multiply_fusion
  165.4 1.6 copy.36
  167.0 51.9 %reduce-scatter.2.cloned.1.call-done = f32[128,2048]{1,0:T(8,128)} async-done(((f32[1024,2048]{1,0:T(8,128)}), f32[128,2048]{1,0:T(8,128)}) %reduce-scatter.2.cloned.1.call-update) | async-done | bytes 1048592 | tf_op jit(solution)/shard_map/reduce_scatter | solution.py:43
  218.9 2.1 fusion
  221.0 2.0 copy.32
  (15 shorter events, 0.1 us)
Async XLA Ops:
  6.5 123.3 %copy-start = (bf16[1024,1024]{1,0:T(8,128)(2,1)S(1)}, bf16[1024,1024]{1,0:T(8,128)(2,1)}, u32[]{:S(2)}) copy-start(bf16[1024,1024]{1,0:T(8,128)(2,1)} %param.7) | copy-start | bytes 6291460
  6.5 4.3 %copy-start.2 = (bf16[16,64,128]{2,1,0:T(8,128)(2,1)S(1)}, bf16[16,64,128]{2,1,0:T(8,128)(2,1)}, u32[]{:S(2)}) copy-start(bf16[16,64,128]{2,1,0:T(8,128)(2,1)} %param.9) | copy-start | bytes 786436
  17.4 11.9 %copy-start.4 = (u32[256]{0:T(256)S(1)}, u32[256]{0:T(256)}, u32[]{:S(2)}) copy-start(u32[256]{0:T(256)} %constant.13) | copy-start | bytes 3076
  17.4 13.1 %copy-start.3 = (s32[4]{0:T(128)S(1)}, s32[4]{0:T(128)}, u32[]{:S(2)}) copy-start(s32[4]{0:T(128)} %param.10) | copy-start | bytes 52
  17.4 71.1 %copy-start.1 = (s32[512]{0:T(512)S(1)}, s32[512]{0:T(512)}, u32[]{:S(2)}) copy-start(s32[512]{0:T(512)} %param.11) | copy-start | bytes 6148
  17.4 72.4 %all-to-all-start = ((bf16[32,16,18,128]{3,1,2,0:T(8,128)(2,1)}), bf16[32,16,18,128]{3,1,2,0:T(8,128)(2,1)}, u32[]{:S(2)}, u32[]{:S(2)}) async-start(bf16[32,16,18,128]{3,1,2,0:T(8,128)(2,1)} %copy.24), calls=%async_computation.1 | async-start | bytes 4718592 | tf_op jit(solution)/shard_map/all_to_all | solution.py:33
  29.2 132.1 %all-gather.3.cloned.1.call-start = ((), (), s32[]{:S(2)}) async-start(), calls=%async_computation.4 | async-start | bytes 4718592 | tf_op jit(solution)/shard_map/all_gather | solution.py:53
  129.6 89.3 %reduce-scatter.2.cloned.1.call-start = ((), (), s32[]{:S(2)}) async-start(), calls=%async_computation.3 | async-start | bytes 9437184 | tf_op jit(solution)/shard_map/reduce_scatter | solution.py:43
Sparse Core Ops, SparseCore 0:
  129.7 31.5 all-gather.2
  163.9 54.9 reduce-scatter.1
